TPU v7x, 256 devices: a whole 4x4x8 slice. The times are simulated.
256 devices in a mesh: dp: 4 (over x), expert: 64 (over z, y, core).
Axes of the slice: x: 4, y: 4, z: 8, core: 2. Of those that a mesh axis runs over, the one named last changes fastest.
Arguments:
- cell_table: bfloat16 [524288, 256], P(('dp', 'expert')), may hold values from -6 to 6
- sample_index: int32 [262144], P(('dp', 'expert')), may hold values from 0 to 2047
- region: int32 [262144, 1], P(('dp', 'expert')), may hold values from 0 to 63; in each aligned block of 1024 rows (0 to 1023, 1024 to 2047, ...) at most 32 rows name the same one
- targets: bfloat16 [262144, 256], P(('dp', 'expert')), may hold values from -6 to 6
- trunk_weight: bfloat16 [256, 256], replicated, may hold values from -0.375 to 0.375
- expert_params: float32 [64, 2, 256, 2048], P('expert', None, None, 'dp'), may hold values from -0.375 to 0.375
- first_moment: float32 [64, 2, 256, 2048], P('expert', None, None, 'dp'), may hold values from -4 to 4
- second_moment: float32 [64, 2, 256, 2048], P('expert', None, None, 'dp'), may hold values from 0.05 to 1
Outputs:
- trunk_grad: float32 [256, 256], replicated
- row_loss: float32 [262144], P(('dp', 'expert'))
- new_params: float32 [64, 2, 256, 2048], P('expert', None, None, 'dp')
- new_first: float32 [64, 2, 256, 2048], P('expert', None, None, 'dp')
- new_second: float32 [64, 2, 256, 2048], P('expert', None, None, 'dp')
Inputs may be any that keep to these rules, and one draw needn't show every extreme that they name: In the 1024 rows of one device no region is named more than 32 times; some region exactly 32 times. `sample_index`: indexes the rows of the same device's block of cell_table.
All inputs are finite; a program needn't handle non-finite values.
Results may differ from a plain program's by a relative error of at most 0.0044.
Values may be sent and summed in bfloat16 or wider, within the bound.
A program may use at most 128 MiB of HBM per device.

v0:
```python
import jax
import jax.numpy as jnp
from jax import lax
from jax.sharding import PartitionSpec as P

loss_scale = 1.0 / 32.0
beta_one = 0.9
beta_two = 0.999
learn_rate = 0.05
adam_eps = 1e-08
adam_step = 10


def silu_slope(values):
    sigma = jax.nn.sigmoid(values)
    return sigma * (1.0 + values * (1.0 - sigma))


def adam_update(params, first, second, grads):
    first_new = beta_one * first + (1.0 - beta_one) * grads
    second_new = beta_two * second + (1.0 - beta_two) * grads * grads
    first_hat = first_new / (1.0 - beta_one**adam_step)
    second_hat = second_new / (1.0 - beta_two**adam_step)
    return (
        params - learn_rate * first_hat / (jnp.sqrt(second_hat) + adam_eps),
        first_new,
        second_new,
    )


def on_device(
    cell_table,
    sample_index,
    region,
    targets,
    trunk_weight,
    expert_params,
    first_moment,
    second_moment,
):
    rows = sample_index.shape[0]
    width = cell_table.shape[1]
    experts = lax.axis_size("expert")
    capacity = 2 * rows // experts
    features = jnp.take(cell_table, sample_index, axis=0)
    routed = region[:, 0]
    onehot = (routed[:, None] == jnp.arange(experts, dtype=jnp.int32)[None, :]).astype(jnp.int32)
    slots = jnp.sum(jnp.cumsum(onehot, axis=0) * onehot, axis=1) - 1
    places = routed * capacity + slots
    gathered = lax.all_gather(expert_params.astype(jnp.bfloat16), "dp", axis=3, tiled=True)
    w_up = gathered[0, 0]
    w_down = gathered[0, 1]
    payload = jnp.concatenate([features, targets], axis=1)
    packed = jnp.zeros((experts * capacity, 2 * width), jnp.bfloat16).at[places].set(payload)
    arrived = lax.all_to_all(
        packed.reshape(experts, capacity, 2 * width),
        "expert",
        split_axis=0,
        concat_axis=0,
        tiled=True,
    ).reshape(-1, 2 * width)
    feats = arrived[:, :width]
    there = arrived[:, width:]
    trunk_pre = jnp.dot(feats, trunk_weight, preferred_element_type=jnp.float32)
    trunk_out = (feats.astype(jnp.float32) + jax.nn.silu(trunk_pre)).astype(jnp.bfloat16)
    up_pre = jnp.dot(trunk_out, w_up, preferred_element_type=jnp.float32)
    hidden = jax.nn.silu(up_pre).astype(jnp.bfloat16)
    predicted = lax.dot_general(
        hidden, w_down, (((1,), (1,)), ((), ())), preferred_element_type=jnp.float32
    )
    errors = predicted - there.astype(jnp.float32)
    losses = jnp.sum(errors * errors, axis=1) * (0.5 * loss_scale)
    scaled = (errors * loss_scale).astype(jnp.bfloat16)
    back = lax.all_to_all(
        losses.reshape(experts, capacity), "expert", split_axis=0, concat_axis=0, tiled=True
    )
    row_loss = back.reshape(-1)[places]
    grad_down = lax.dot_general(
        scaled, hidden, (((0,), (0,)), ((), ())), preferred_element_type=jnp.float32
    )
    hidden_grad = jnp.dot(scaled, w_down, preferred_element_type=jnp.float32)
    pre_grad = (hidden_grad * silu_slope(up_pre)).astype(jnp.bfloat16)
    grad_up = lax.dot_general(
        trunk_out, pre_grad, (((0,), (0,)), ((), ())), preferred_element_type=jnp.float32
    )
    row_grad = lax.dot_general(
        pre_grad, w_up, (((1,), (1,)), ((), ())), preferred_element_type=jnp.float32
    ).astype(jnp.bfloat16)
    trunk_slope = (row_grad.astype(jnp.float32) * silu_slope(trunk_pre)).astype(jnp.bfloat16)
    trunk_local = lax.dot_general(
        feats, trunk_slope, (((0,), (0,)), ((), ())), preferred_element_type=jnp.float32
    )
    trunk_grad = lax.psum(trunk_local, ("dp", "expert"))
    grads = jnp.stack([grad_up, grad_down])[None]
    grad_shard = lax.psum_scatter(grads, "dp", scatter_dimension=3, tiled=True)
    new_params, new_first, new_second = adam_update(
        expert_params, first_moment, second_moment, grad_shard
    )
    return (trunk_grad, row_loss, new_params, new_first, new_second)


def solution(mesh):
    placed = (
        P(("dp", "expert"), None),
        P(("dp", "expert")),
        P(("dp", "expert"), None),
        P(("dp", "expert"), None),
        P(),
        P("expert", None, None, "dp"),
        P("expert", None, None, "dp"),
        P("expert", None, None, "dp"),
    )
    return jax.shard_map(
        on_device,
        mesh=mesh,
        in_specs=placed,
        out_specs=(
            P(),
            P(("dp", "expert")),
            P("expert", None, None, "dp"),
            P("expert", None, None, "dp"),
            P("expert", None, None, "dp"),
        ),
        check_vma=False,
    )
```

profile of v0, /device:TPU:2, one launch (start us, length us, event | category | flops | bytes accessed | tf_op | source)
XLA Modules:
  0.0 451.5 jit_solution(14048339895175946293)
XLA Ops:
  7.2 0.0 copy-start
  7.2 0.0 copy-start.6
  7.2 0.8 fusion.17
  8.0 0.7 compare_and_fusion
  8.7 0.7 fusion.16
  9.4 18.0 %reduce-window.6 = s32[64,8,128]{2,1,0:T(8,128)S(1)} reduce-window(s32[64,8,128]{2,1,0:T(8,128)S(1)} %fusion.16, s32[]{:T(128)} %constant.20.clone.1), window={size=1x1x128 pad=0_0x0_0x127_0}, to_apply=%region_0.1 | reduce-window | flops 8323072 | bytes 524292 | tf_op jit(solution)/shard_map/reduce-window
  27.4 0.1 slice.28
  27.5 0.1 copy.17
  27.7 0.1 copy.18
  27.8 0.1 broadcast_add_fusion
  27.9 0.0 copy-done.6
  27.9 0.1 fusion.15
  28.1 0.0 copy-start.4
  28.1 3.9 gather_fusion
  32.0 0.2 broadcast_select_fusion
  32.2 0.0 copy-done.4
  32.2 6.7 %scatter_custom_fusion = bf16[2048,512]{1,0:T(8,128)(2,1)} fusion(s32[1024]{0:T(1024)S(1)} %bitcast.54, bf16[1024,256]{1,0:T(8,128)(2,1)S(1)} %copy-done.4, bf16[]{:T(256)} %constant.67, bf16[1024,256]{1,0:T(8,128)(2,1)S(1)} %broadcast_select_fusion, bf16[]{:T(256)} %constant.18.clone.1), kind=kCustom, calls=%fused_computation.22 | custom fusion | flops 2097152 | bytes 3145732 | tf_op jit(solution)/shard_map/scatter | solution.py:54
  38.9 12.1 %all-to-all-start = ((bf16[64,32,512]{2,1,0:T(8,128)(2,1)}), bf16[64,32,512]{2,1,0:T(8,128)(2,1)S(1)}, u32[]{:S(2)}, u32[]{:S(2)}) async-start(bf16[64,32,512]{2,1,0:T(8,128)(2,1)} %bitcast.6), calls=%async_computation | async-start | bytes 4194304 | tf_op jit(solution)/shard_map/all_to_all | solution.py:55
  51.0 0.0 copy-start.5
  51.1 0.0 all-gather.2.cloned.1.call-start
  51.1 2.1 convert_element_type.38
  53.2 0.0 all-gather.2.cloned.1.call-update
  53.2 0.2 reduce-scatter.2.cloned.1.call-start
  53.5 48.9 %all-to-all-done = bf16[64,32,512]{2,1,0:T(8,128)(2,1)S(1)} async-done(((bf16[64,32,512]{2,1,0:T(8,128)(2,1)}), bf16[64,32,512]{2,1,0:T(8,128)(2,1)S(1)}, u32[]{:S(2)}, u32[]{:S(2)}) %all-to-all-start) | async-done | bytes 2097184 | tf_op jit(solution)/shard_map/all_to_all | solution.py:55
  102.4 1.7 fusion.12
  104.2 10.1 %multiply_convert_fusion.1 = (bf16[2048,2048]{1,0:T(8,128)(2,1)S(1)}, f32[2048,2048]{1,0:T(8,128)}) fusion(bf16[1,2,256,2048]{3,2,1,0:T(8,128)(2,1)} %all-gather.2.cloned.1.call-done, f32[2048,256]{1,0:T(8,128)} %fusion.12, bf16[2048,512]{1,0:T(8,128)(2,1)S(1)} %bitcast.46), kind=kOutput, calls=%fused_computation.4 | convolution fusion | flops 2172125184 | bytes 29360128 | tf_op jit(solution)/shard_map/dot_general | solution.py:66
  114.3 2.6 multiply_reduce_fusion
  116.9 2.3 convolution_bitcast_fusion
  119.3 13.3 %multiply_convert_fusion = bf16[2048,2048]{1,0:T(8,128)(2,1)} fusion(f32[2048,2048]{1,0:T(8,128)} %get-tuple-element.9, bf16[1,2,256,2048]{3,2,1,0:T(8,128)(2,1)S(1)} %copy-done.7, f32[2048,256]{1,0:T(8,128)S(1)} %get-tuple-element.11), kind=kOutput, calls=%fused_computation.3 | convolution fusion | flops 2186280960 | bytes 28311552 | tf_op jit(solution)/shard_map/dot_general | solution.py:81
  132.6 0.0 copy-done.2
  132.6 5.8 %convolution_bitcast_fusion.1 = f32[1,256,2048]{2,1,0:T(8,128)S(1)} fusion(bf16[2048,2048]{1,0:T(8,128)(2,1)} %multiply_convert_fusion, f32[2048,256]{1,0:T(8,128)S(1)} %copy-done.2, bf16[2048,512]{1,0:T(8,128)(2,1)S(1)} %bitcast.48), kind=kOutput, calls=%fused_computation.8 | convolution fusion | flops 2151153664 | bytes 13631488 | tf_op jit(solution)/shard_map/dot_general | solution.py:83
  138.4 2.2 maximum_bitcast_fusion
  140.6 0.0 reduce-scatter.2.cloned.1.call-update
  140.7 0.7 mul.111
  141.3 5.6 %all-to-all-start.1 = ((f32[64,1,32]{2,1,0:T(1,128)}), f32[64,1,32]{2,1,0:T(1,128)S(1)}, u32[]{:S(2)}, u32[]{:S(2)}) async-start(f32[64,1,32]{2,1,0:T(1,128)} %bitcast.10), calls=%async_computation.1 | async-start | bytes 65536 | tf_op jit(solution)/shard_map/all_to_all | solution.py:74
  146.9 0.0 all-reduce.2.cloned.1.call-start
  147.0 9.0 %fusion.9 = f32[256,256]{1,0:T(8,128)} fusion(bf16[2048,2048]{1,0:T(8,128)(2,1)} %multiply_convert_fusion, f32[2048,256]{1,0:T(8,128)} %fusion.12, bf16[1,2,256,2048]{3,2,1,0:T(8,128)(2,1)} %all-gather.2.cloned.1.call-done, bf16[2048,512]{1,0:T(8,128)(2,1)S(1)} %bitcast.49), kind=kOutput, calls=%fused_computation.29 | convolution fusion | flops 2421686272 | bytes 12845056 | tf_op jit(solution)/shard_map/dot_general | solution.py:90
  155.9 0.0 all-reduce.2.cloned.1.call-update
  156.0 0.5 all-to-all-done.1
  156.4 0.5 broadcast.88
  157.0 0.7 reduce.3
  157.7 0.1 reshape.69
  157.8 10.5 %gather_fusion.1 = f32[1024]{0:T(1024)} fusion(f32[2048]{0:T(1024)S(1)} %reshape.69, s32[1024]{0:T(1024)S(1)} %broadcast_clamp_fusion), kind=kCustom, calls=%fused_computation.1 | custom fusion | bytes 12288 | tf_op jit(solution)/shard_map/gather | solution.py:77
  168.3 16.8 %reduce-scatter.2.cloned.1.call-done = f32[1,2,256,512]{3,2,1,0:T(8,128)} async-done(((f32[1,2,256,2048]{3,2,1,0:T(8,128)}), f32[1,2,256,512]{3,2,1,0:T(8,128)}) %reduce-scatter.2.cloned.1.call-update) | async-done | bytes 1048592 | tf_op jit(solution)/shard_map/reduce_scatter | solution.py:95
  185.1 0.0 copy-done.1
  185.1 3.7 divide_subtract_fusion
  188.8 254.6 %all-reduce.2.cloned.1.call-done = f32[256,256]{1,0:T(8,128)} async-done(((f32[256,256]{1,0:T(8,128)}), f32[256,256]{1,0:T(8,128)}) %all-reduce.2.cloned.1.call-update) | async-done | bytes 262160 | tf_op jit(solution)/shard_map/psum | solution.py:93
  443.3 1.7 copy.25
  (15 shorter events, 0.1 us)
Async XLA Ops:
  7.2 20.9 %copy-start = (bf16[2048,256]{1,0:T(8,128)(2,1)S(1)}, bf16[2048,256]{1,0:T(8,128)(2,1)}, u32[]{:S(2)}) copy-start(bf16[2048,256]{1,0:T(8,128)(2,1)} %param.8) | copy-start | bytes 3145732
  7.2 20.8 %copy-start.6 = (s32[1024,1]{0,1:T(1,128)S(1)}, s32[1024,1]{0,1:T(1,128)}, u32[]{:S(2)}) copy-start(s32[1024,1]{0,1:T(1,128)} %param.10) | copy-start | bytes 12292
  28.1 4.2 copy-start.4
  38.9 63.5 %all-to-all-start = ((bf16[64,32,512]{2,1,0:T(8,128)(2,1)}), bf16[64,32,512]{2,1,0:T(8,128)(2,1)S(1)}, u32[]{:S(2)}, u32[]{:S(2)}) async-start(bf16[64,32,512]{2,1,0:T(8,128)(2,1)} %bitcast.6), calls=%async_computation | async-start | bytes 4194304 | tf_op jit(solution)/shard_map/all_to_all | solution.py:55
  51.0 51.4 %copy-start.5 = (bf16[256,256]{1,0:T(8,128)(2,1)S(1)}, bf16[256,256]{1,0:T(8,128)(2,1)}, u32[]{:S(2)}) copy-start(bf16[256,256]{1,0:T(8,128)(2,1)} %param.12) | copy-start | bytes 393220
  51.1 53.1 %all-gather.2.cloned.1.call-start = ((), (), s32[]{:S(2)}) async-start(), calls=%async_computation.3 | async-start | bytes 2621440 | tf_op jit(solution)/shard_map/all_gather | solution.py:50
  53.2 131.8 %reduce-scatter.2.cloned.1.call-start = ((), (), s32[]{:S(2)}) async-start(), calls=%async_computation.5 | async-start | bytes 5242880 | tf_op jit(solution)/shard_map/reduce_scatter | solution.py:95
  104.1 10.1 %copy-start.7 = (bf16[1,2,256,2048]{3,2,1,0:T(8,128)(2,1)S(1)}, bf16[1,2,256,2048]{3,2,1,0:T(8,128)(2,1)}, u32[]{:S(2)}) copy-start(bf16[1,2,256,2048]{3,2,1,0:T(8,128)(2,1)} %all-gather.2.cloned.1.call-done) | copy-start | bytes 6291460
  119.3 13.3 %copy-start.2 = (f32[2048,256]{1,0:T(8,128)S(1)}, f32[2048,256]{1,0:T(8,128)}, u32[]{:S(2)}) copy-start(f32[2048,256]{1,0:T(8,128)} %fusion.12) | copy-start | bytes 6291460
  141.3 15.1 %all-to-all-start.1 = ((f32[64,1,32]{2,1,0:T(1,128)}), f32[64,1,32]{2,1,0:T(1,128)S(1)}, u32[]{:S(2)}, u32[]{:S(2)}) async-start(f32[64,1,32]{2,1,0:T(1,128)} %bitcast.10), calls=%async_computation.1 | async-start | bytes 65536 | tf_op jit(solution)/shard_map/all_to_all | solution.py:74
  146.9 296.4 %all-reduce.2.cloned.1.call-start = ((), (), s32[]{:S(2)}) async-start(), calls=%async_computation.4 | async-start | bytes 524288 | tf_op jit(solution)/shard_map/psum | solution.py:93
  157.8 27.3 %copy-start.1 = (f32[1,2,256,512]{3,2,1,0:T(8,128)S(1)}, f32[1,2,256,512]{3,2,1,0:T(8,128)}, u32[]{:S(2)}) copy-start(f32[1,2,256,512]{3,2,1,0:T(8,128)} %param.13) | copy-start | bytes 3145732
  157.8 27.3 %copy-start.3 = (f32[1,2,256,512]{3,2,1,0:T(8,128)S(1)}, f32[1,2,256,512]{3,2,1,0:T(8,128)}, u32[]{:S(2)}) copy-start(f32[1,2,256,512]{3,2,1,0:T(8,128)} %param.14) | copy-start | bytes 3145732
Sparse Core Ops, SparseCore 0:
  54.3 33.5 all-gather.1
  140.7 44.3 reduce-scatter.1
  192.0 251.2 all-reduce.1
where the time goes:
time: 452 us
  waiting for transfers between devices  321 us (71%)
  matrix products  44.9 us (10%)
  other arithmetic  36.1 us (8%)
  starting transfers between devices  18 us (4%)
  local copies, waits for them, and re-layouts  17.8 us (4%)
  between operations  13.9 us (3%)
    psum x1, waiting for transfers between devices, on_device(): trunk_grad = lax.psum(trunk_local, ('dp', 'expert'))  255 us
    all_to_all x1, waiting for transfers between devices, on_device(): lax.all_to_all(packed.reshape(experts, capacity, 2 * width), 'expert', sp...  48.9 us
    another operation x3, other arithmetic  18.2 us
    reduce_scatter x1, waiting for transfers between devices, on_device(): grad_shard = lax.psum_scatter(grads, 'dp', scatter_dimension=3, tiled=True)  16.8 us
    dot_general x1, matrix products, on_device(): hidden_grad = jnp.dot(scaled, w_down, preferred_element_type=jnp.float32)  13.3 us
    all_to_all x1, starting transfers between devices, on_device(): lax.all_to_all(packed.reshape(experts, capacity, 2 * width), 'expert', sp...  12.1 us
    gather x1, local copies, waits for them, and re-layouts, on_device(): row_loss = back.reshape(-1)[places]  10.5 us
    dot_general x1, matrix products, on_device(): up_pre = jnp.dot(trunk_out, w_up, preferred_element_type=jnp.float32)  10.1 us
  transfers between devices with their start and end apart: 5, of which 4 were waited for; matrix products, arithmetic and copies ran while one was open for 6% of the time, Pallas kernels for 0%

commit v1 on v0

--- a/solution.py
+++ b/solution.py
@@ -90,7 +90,7 @@
     trunk_local = lax.dot_general(
         feats, trunk_slope, (((0,), (0,)), ((), ())), preferred_element_type=jnp.float32
     )
-    trunk_grad = lax.psum(trunk_local, ("dp", "expert"))
+    trunk_grad = lax.psum(lax.psum(trunk_local, "dp"), "expert")
     grads = jnp.stack([grad_up, grad_down])[None]
     grad_shard = lax.psum_scatter(grads, "dp", scatter_dimension=3, tiled=True)
     new_params, new_first, new_second = adam_update(

time: 452 us -> 432 us (0.956)
  waiting for transfers between devices: 321 us -> 296 us
    psum x1 -> x2, waiting for transfers between devices: 255 us -> 185 us  [on_device(): trunk_grad = lax.psum(lax.psum(trunk_local, 'dp'), 'expert')]
    reduce_scatter x1, waiting for transfers between devices: 16.8 us -> 52.4 us  [on_device(): grad_shard = lax.psum_scatter(grads, 'dp', scatter_dimension=3, tiled=True)]
    all_to_all x1, waiting for transfers between devices: 0.48 us -> 9.46 us  [on_device(): lax.all_to_all(losses.reshape(experts, capacity), 'expert', split_axis=0,...]
  transfers between devices with their start and end apart: 5 -> 6, of which waited for: 4 -> 5; matrix products, arithmetic and copies ran while one was open for 6% -> 6% of each run, Pallas kernels for 0% -> 0%
where the time goes in v1:
time: 432 us; the launch traced here: 429 us
  waiting for transfers between devices  296 us (69%)
  matrix products  46 us (11%)
  other arithmetic  37.8 us (9%)
  local copies, waits for them, and re-layouts  17.8 us (4%)
  starting transfers between devices  17.8 us (4%)
  between operations  14 us (3%)
    psum x2, waiting for transfers between devices, on_device(): trunk_grad = lax.psum(lax.psum(trunk_local, 'dp'), 'expert')  185 us
    reduce_scatter x1, waiting for transfers between devices, on_device(): grad_shard = lax.psum_scatter(grads, 'dp', scatter_dimension=3, tiled=True)  52.4 us
    all_to_all x1, waiting for transfers between devices, on_device(): lax.all_to_all(packed.reshape(experts, capacity, 2 * width), 'expert', sp...  48.9 us
    another operation x3, other arithmetic  18.2 us
    dot_general x1, matrix products, on_device(): hidden_grad = jnp.dot(scaled, w_down, preferred_element_type=jnp.float32)  13.3 us
    all_to_all x1, starting transfers between devices, on_device(): lax.all_to_all(packed.reshape(experts, capacity, 2 * width), 'expert', sp...  12.1 us
    gather x1, local copies, waits for them, and re-layouts, on_device(): row_loss = back.reshape(-1)[places]  10.5 us
    dot_general x1, matrix products, on_device(): up_pre = jnp.dot(trunk_out, w_up, preferred_element_type=jnp.float32)  10.2 us
  transfers between devices with their start and end apart: 6, of which 5 were waited for; matrix products, arithmetic and copies ran while one was open for 6% of the time, Pallas kernels for 0%

profile of v1, /device:TPU:2, one launch (start us, length us, event | category | flops | bytes accessed | tf_op | source)
XLA Modules:
  0.0 429.3 jit_solution(12817080552622944949)
XLA Ops:
  7.2 0.0 copy-start
  7.2 0.0 copy-start.8
  7.2 0.8 fusion.17
  8.0 0.7 compare_and_fusion
  8.7 0.7 fusion.16
  9.4 18.0 %reduce-window.6 = s32[64,8,128]{2,1,0:T(8,128)S(1)} reduce-window(s32[64,8,128]{2,1,0:T(8,128)S(1)} %fusion.16, s32[]{:T(128)} %constant.20.clone.1), window={size=1x1x128 pad=0_0x0_0x127_0}, to_apply=%region_0.1 | reduce-window | flops 8323072 | bytes 524292 | tf_op jit(solution)/shard_map/reduce-window
  27.4 0.1 slice.28
  27.5 0.1 copy.17
  27.7 0.1 copy.18
  27.8 0.1 broadcast_add_fusion
  27.9 0.1 fusion.15
  28.1 0.0 copy-start.6
  28.1 3.9 gather_fusion
  32.0 0.2 broadcast_select_fusion
  32.2 0.0 copy-done.6
  32.2 6.7 %scatter_custom_fusion = bf16[2048,512]{1,0:T(8,128)(2,1)} fusion(s32[1024]{0:T(1024)S(1)} %bitcast.54, bf16[1024,256]{1,0:T(8,128)(2,1)S(1)} %copy-done.6, bf16[]{:T(256)} %constant.67, bf16[1024,256]{1,0:T(8,128)(2,1)S(1)} %broadcast_select_fusion, bf16[]{:T(256)} %constant.18.clone.1), kind=kCustom, calls=%fused_computation.22 | custom fusion | flops 2097152 | bytes 3145732 | tf_op jit(solution)/shard_map/scatter | solution.py:54
  38.9 12.1 %all-to-all-start = ((bf16[64,32,512]{2,1,0:T(8,128)(2,1)}), bf16[64,32,512]{2,1,0:T(8,128)(2,1)S(1)}, u32[]{:S(2)}, u32[]{:S(2)}) async-start(bf16[64,32,512]{2,1,0:T(8,128)(2,1)} %bitcast.6), calls=%async_computation | async-start | bytes 4194304 | tf_op jit(solution)/shard_map/all_to_all | solution.py:55
  51.0 0.0 copy-start.7
  51.1 0.0 all-gather.2.cloned.1.call-start
  51.1 2.1 convert_element_type.38
  53.2 0.0 all-gather.2.cloned.1.call-update
  53.2 0.2 all-reduce.3.cloned.1.call-start
  53.5 48.9 %all-to-all-done = bf16[64,32,512]{2,1,0:T(8,128)(2,1)S(1)} async-done(((bf16[64,32,512]{2,1,0:T(8,128)(2,1)}), bf16[64,32,512]{2,1,0:T(8,128)(2,1)S(1)}, u32[]{:S(2)}, u32[]{:S(2)}) %all-to-all-start) | async-done | bytes 2097184 | tf_op jit(solution)/shard_map/all_to_all | solution.py:55
  102.4 2.0 fusion.12
  104.4 10.2 %multiply_convert_fusion.1 = (bf16[2048,2048]{1,0:T(8,128)(2,1)S(1)}, f32[2048,2048]{1,0:T(8,128)}) fusion(bf16[1,2,256,2048]{3,2,1,0:T(8,128)(2,1)} %all-gather.2.cloned.1.call-done, f32[2048,256]{1,0:T(8,128)} %fusion.12, bf16[2048,512]{1,0:T(8,128)(2,1)S(1)} %bitcast.46), kind=kOutput, calls=%fused_computation.4 | convolution fusion | flops 2172125184 | bytes 29360128 | tf_op jit(solution)/shard_map/dot_general | solution.py:66
  114.6 2.6 multiply_reduce_fusion
  117.2 2.3 convolution_bitcast_fusion
  119.6 13.3 %multiply_convert_fusion = bf16[2048,2048]{1,0:T(8,128)(2,1)} fusion(f32[2048,2048]{1,0:T(8,128)} %get-tuple-element.9, bf16[1,2,256,2048]{3,2,1,0:T(8,128)(2,1)S(1)} %copy-done.9, f32[2048,256]{1,0:T(8,128)S(1)} %get-tuple-element.11), kind=kOutput, calls=%fused_computation.3 | convolution fusion | flops 2186280960 | bytes 28311552 | tf_op jit(solution)/shard_map/dot_general | solution.py:81
  132.9 7.1 %convolution_bitcast_fusion.1 = f32[1,256,2048]{2,1,0:T(8,128)} fusion(bf16[2048,2048]{1,0:T(8,128)(2,1)} %multiply_convert_fusion, f32[2048,256]{1,0:T(8,128)S(1)} %copy-done.4, bf16[2048,512]{1,0:T(8,128)(2,1)S(1)} %bitcast.49), kind=kOutput, calls=%fused_computation.8 | convolution fusion | flops 2151153664 | bytes 13631488 | tf_op jit(solution)/shard_map/dot_general | solution.py:83
  140.0 8.5 %fusion.9 = f32[256,256]{1,0:T(8,128)} fusion(bf16[2048,2048]{1,0:T(8,128)(2,1)} %multiply_convert_fusion, f32[2048,256]{1,0:T(8,128)} %fusion.12, bf16[1,2,256,2048]{3,2,1,0:T(8,128)(2,1)} %all-gather.2.cloned.1.call-done, bf16[2048,512]{1,0:T(8,128)(2,1)} %bitcast.48), kind=kOutput, calls=%fused_computation.29 | convolution fusion | flops 2421686272 | bytes 12845056 | tf_op jit(solution)/shard_map/dot_general | solution.py:90
  148.5 0.0 all-reduce.3.cloned.1.call-update
  148.5 0.0 reduce-scatter.2.cloned.1.call-start
  148.6 3.9 maximum_bitcast_fusion
  152.5 0.0 reduce-scatter.2.cloned.1.call-update
  152.5 0.7 mul.111
  153.2 5.3 %all-to-all-start.1 = ((f32[64,1,32]{2,1,0:T(1,128)}), f32[64,1,32]{2,1,0:T(1,128)S(1)}, u32[]{:S(2)}, u32[]{:S(2)}) async-start(f32[64,1,32]{2,1,0:T(1,128)} %bitcast.10), calls=%async_computation.1 | async-start | bytes 65536 | tf_op jit(solution)/shard_map/all_to_all | solution.py:74
  158.5 0.0 all-reduce.5.cloned.1.call-start
  158.6 9.5 %all-to-all-done.1 = f32[64,1,32]{2,1,0:T(1,128)S(1)} async-done(((f32[64,1,32]{2,1,0:T(1,128)}), f32[64,1,32]{2,1,0:T(1,128)S(1)}, u32[]{:S(2)}, u32[]{:S(2)}) %all-to-all-start.1) | async-done | bytes 8224 | tf_op jit(solution)/shard_map/all_to_all | solution.py:74
  168.1 0.5 broadcast.88
  168.6 0.7 reduce.3
  169.3 0.1 reshape.69
  169.4 10.5 %gather_fusion.1 = f32[1024]{0:T(1024)} fusion(f32[2048]{0:T(1024)S(1)} %reshape.69, s32[1024]{0:T(1024)S(1)} %broadcast_clamp_fusion), kind=kCustom, calls=%fused_computation.1 | custom fusion | bytes 12288 | tf_op jit(solution)/shard_map/gather | solution.py:77
  179.9 10.6 %all-reduce.3.cloned.1.call-done = f32[256,256]{1,0:T(8,128)} async-done(((f32[256,256]{1,0:T(8,128)}), f32[256,256]{1,0:T(8,128)}) %all-reduce.3.cloned.1.call-update) | async-done | bytes 262160 | tf_op jit(solution)/shard_map/psum | solution.py:93
  190.5 0.0 all-reduce.5.cloned.1.call-update
  190.5 52.4 %reduce-scatter.2.cloned.1.call-done = f32[1,2,256,512]{3,2,1,0:T(8,128)} async-done(((f32[1,2,256,2048]{3,2,1,0:T(8,128)}), f32[1,2,256,512]{3,2,1,0:T(8,128)}) %reduce-scatter.2.cloned.1.call-update) | async-done | bytes 1048592 | tf_op jit(solution)/shard_map/reduce_scatter | solution.py:95
  242.9 3.7 divide_subtract_fusion
  246.6 174.5 %all-reduce.5.cloned.1.call-done = f32[256,256]{1,0:T(8,128)} async-done(((f32[256,256]{1,0:T(8,128)}), f32[256,256]{1,0:T(8,128)}) %all-reduce.5.cloned.1.call-update) | async-done | bytes 262160 | tf_op jit(solution)/shard_map/psum | solution.py:93
  421.1 1.7 copy.26
  (22 shorter events, 0.1 us)
Async XLA Ops:
  7.2 20.9 %copy-start = (bf16[2048,256]{1,0:T(8,128)(2,1)S(1)}, bf16[2048,256]{1,0:T(8,128)(2,1)}, u32[]{:S(2)}) copy-start(bf16[2048,256]{1,0:T(8,128)(2,1)} %param.8) | copy-start | bytes 3145732
  7.2 20.8 %copy-start.8 = (s32[1024,1]{0,1:T(1,128)S(1)}, s32[1024,1]{0,1:T(1,128)}, u32[]{:S(2)}) copy-start(s32[1024,1]{0,1:T(1,128)} %param.10) | copy-start | bytes 12292
  28.1 4.2 copy-start.6
  38.9 63.5 %all-to-all-start = ((bf16[64,32,512]{2,1,0:T(8,128)(2,1)}), bf16[64,32,512]{2,1,0:T(8,128)(2,1)S(1)}, u32[]{:S(2)}, u32[]{:S(2)}) async-start(bf16[64,32,512]{2,1,0:T(8,128)(2,1)} %bitcast.6), calls=%async_computation | async-start | bytes 4194304 | tf_op jit(solution)/shard_map/all_to_all | solution.py:55
  51.0 51.4 %copy-start.7 = (bf16[256,256]{1,0:T(8,128)(2,1)S(1)}, bf16[256,256]{1,0:T(8,128)(2,1)}, u32[]{:S(2)}) copy-start(bf16[256,256]{1,0:T(8,128)(2,1)} %param.12) | copy-start | bytes 393220
  51.1 53.3 %all-gather.2.cloned.1.call-start = ((), (), s32[]{:S(2)}) async-start(), calls=%async_computation.3 | async-start | bytes 2621440 | tf_op jit(solution)/shard_map/all_gather | solution.py:50
  53.2 137.2 %all-reduce.3.cloned.1.call-start = ((), (), s32[]{:S(2)}) async-start(), calls=%async_computation.4 | async-start | bytes 524288 | tf_op jit(solution)/shard_map/psum | solution.py:93
  102.4 12.2 %copy-start.1 = (bf16[64,32,512]{2,1,0:T(8,128)(2,1)}, bf16[64,32,512]{2,1,0:T(8,128)(2,1)S(1)}, u32[]{:S(2)}) copy-start(bf16[64,32,512]{2,1,0:T(8,128)(2,1)S(1)} %all-to-all-done) | copy-start | bytes 6291460
  104.4 10.2 %copy-start.9 = (bf16[1,2,256,2048]{3,2,1,0:T(8,128)(2,1)S(1)}, bf16[1,2,256,2048]{3,2,1,0:T(8,128)(2,1)}, u32[]{:S(2)}) copy-start(bf16[1,2,256,2048]{3,2,1,0:T(8,128)(2,1)} %all-gather.2.cloned.1.call-done) | copy-start | bytes 6291460
  119.5 13.4 %copy-start.2 = (bf16[64,32,512]{2,1,0:T(8,128)(2,1)S(1)}, bf16[64,32,512]{2,1,0:T(8,128)(2,1)}, u32[]{:S(2)}) copy-start(bf16[64,32,512]{2,1,0:T(8,128)(2,1)} %copy-done.1) | copy-start | bytes 6291460
  119.5 13.3 %copy-start.4 = (f32[2048,256]{1,0:T(8,128)S(1)}, f32[2048,256]{1,0:T(8,128)}, u32[]{:S(2)}) copy-start(f32[2048,256]{1,0:T(8,128)} %fusion.12) | copy-start | bytes 6291460
  148.5 94.4 %reduce-scatter.2.cloned.1.call-start = ((), (), s32[]{:S(2)}) async-start(), calls=%async_computation.6 | async-start | bytes 5242880 | tf_op jit(solution)/shard_map/reduce_scatter | solution.py:95
  153.2 14.9 %all-to-all-start.1 = ((f32[64,1,32]{2,1,0:T(1,128)}), f32[64,1,32]{2,1,0:T(1,128)S(1)}, u32[]{:S(2)}, u32[]{:S(2)}) async-start(f32[64,1,32]{2,1,0:T(1,128)} %bitcast.10), calls=%async_computation.1 | async-start | bytes 65536 | tf_op jit(solution)/shard_map/all_to_all | solution.py:74
  158.5 262.6 %all-reduce.5.cloned.1.call-start = ((), (), s32[]{:S(2)}) async-start(), calls=%async_computation.5 | async-start | bytes 524288 | tf_op jit(solution)/shard_map/psum | solution.py:93
  169.4 73.6 %copy-start.3 = (f32[1,2,256,512]{3,2,1,0:T(8,128)S(1)}, f32[1,2,256,512]{3,2,1,0:T(8,128)}, u32[]{:S(2)}) copy-start(f32[1,2,256,512]{3,2,1,0:T(8,128)} %param.13) | copy-start | bytes 3145732
  169.4 73.6 %copy-start.5 = (f32[1,2,256,512]{3,2,1,0:T(8,128)S(1)}, f32[1,2,256,512]{3,2,1,0:T(8,128)}, u32[]{:S(2)}) copy-start(f32[1,2,256,512]{3,2,1,0:T(8,128)} %param.14) | copy-start | bytes 3145732
Sparse Core Ops, SparseCore 0:
  54.3 33.5 all-gather.1
  148.6 41.8 all-reduce.2
  193.2 49.6 reduce-scatter.1
  246.3 174.7 all-reduce.4
